TPU v7x, 32 devices: a whole 2x2x4 slice. The times are simulated.
32 devices in a mesh: dp: 2 (over x), space: 16 (over z, y, core).
Axes of the slice: x: 2, y: 2, z: 4, core: 2. Of those that a mesh axis runs over, the one named last changes fastest.
Arguments:
- tiles_in: bfloat16 [2, 64, 8, 8, 384], P('dp', 'space'), may hold values from -6 to 6
- upstream: bfloat16 [2, 64, 8, 8, 384], P('dp', 'space'), may hold values from -1.1953125 to 1.1953125
- pool_weight: float32 [2, 64], P('dp', 'space'), may hold values from 0.25 to 4
- slide_cot: float32 [2, 384], P('dp'), may hold values from -6 to 6
- adjacency: int32 [2, 64, 8], P('dp', 'space'), may hold values from -1 to 63, as said below
- counts: int32 [2, 16], P('dp', 'space'), may hold values from 1 to 4, as said below
- kernel: float32 [7, 7, 384], replicated, may hold values from -0.875 to 0.875
- norm_gain: float32 [384], replicated, may hold values from 0.5 to 1.5
- w_in: bfloat16 [384, 1536], replicated, may hold values from -0.3125 to 0.3125
- w_out: bfloat16 [1536, 384], replicated, may hold values from -0.15625 to 0.15625
- layer_scale: float32 [384], replicated, may hold values from 0.1 to 1
Outputs:
- embedding: float32 [2, 384], P('dp')
- grad_tiles: bfloat16 [2, 64, 8, 8, 384], P('dp', 'space')
- grad_w_out: float32 [1536, 384], P('space')
- grad_kernel: float32 [7, 7, 384], replicated
Inputs may be any that keep to these rules, and one draw needn't show every extreme that they name: Slots form blocks of 4; block k of a slide is one row of tiles, its live tiles in its first counts slots in column order; the last block of every slide is full, and often another one too. `adjacency`: tiles lie on a grid: entries 0, 4, 5 name live slots of the block before the tile's own, entries 1, 6, 7 of the block after it, entries 2 and 3 of its own block. The lists are mutual (b is the north neighbour of a exactly when a is the south neighbour of b, and likewise for the other directions). Slots that are not live have no neighbours and are named by none.
All inputs are finite; a program needn't handle non-finite values.
Results may differ from a plain program's by a relative error of at most 0.011.
Values may be sent and summed in bfloat16 or wider, within the bound.
No kernel may reach another device: no remote copies, remote signals or barrier semaphores. Data moves between devices by JAX's collectives and lax.ppermute only.
A program may use at most 64 MiB of HBM per device.

v0:
```python
import jax
import jax.numpy as jnp
from jax import lax
from jax.sharding import PartitionSpec as P

sqrt_half = 0.7071067811865476
inv_root_two_pi = 0.3989422804014327


def passed_along(value, axis, steps):
    count = lax.axis_size(axis)
    leading, last = (max(0, -steps), min(count, count - steps))
    return lax.ppermute(value, axis, [(source, source + steps) for source in range(leading, last)])


def depthwise(padded, kernel, tile_side):
    total = jnp.zeros(padded.shape[:1] + (tile_side, tile_side, padded.shape[3]), jnp.float32)
    for row_tap in range(7):
        for col_tap in range(7):
            window = padded[
                :, row_tap : row_tap + tile_side, col_tap : col_tap + tile_side, :
            ].astype(jnp.float32)
            total = total + window * kernel[row_tap, col_tap]
    return total


def pick(source, wanted, offset):
    valid = wanted >= 0
    index = jnp.clip(wanted - offset, 0, source.shape[0] - 1)
    chosen = jnp.take(source, index, axis=0)
    return jnp.where(valid[:, None, None, None], chosen, jnp.zeros_like(chosen))


def frame(
    own, north_rows, south_rows, right_cols, left_cols, wanted, north_base, own_base, south_base
):
    tile_side = own.shape[1]
    upper = jnp.concatenate(
        [
            pick(north_rows, wanted[:, 4], north_base)[:, :, tile_side - 3 :],
            pick(north_rows, wanted[:, 0], north_base),
            pick(north_rows, wanted[:, 5], north_base)[:, :, :3],
        ],
        axis=2,
    )
    middle = jnp.concatenate(
        [pick(right_cols, wanted[:, 2], own_base), own, pick(left_cols, wanted[:, 3], own_base)],
        axis=2,
    )
    lower = jnp.concatenate(
        [
            pick(south_rows, wanted[:, 6], south_base)[:, :, tile_side - 3 :],
            pick(south_rows, wanted[:, 1], south_base),
            pick(south_rows, wanted[:, 7], south_base)[:, :, :3],
        ],
        axis=2,
    )
    return jnp.concatenate([upper, middle, lower], axis=1)


def block_pass(
    padded, own, upstream, pool_weight, live, slide_cot, kernel, norm_gain, w_in, w_out, layer_scale
):
    tile_side = own.shape[1]
    channels = own.shape[3]
    conv_out = depthwise(padded, kernel, tile_side)
    centred = conv_out - jnp.mean(conv_out, axis=-1, keepdims=True)
    inv_std = lax.rsqrt(jnp.mean(centred * centred, axis=-1, keepdims=True) + 1e-06)
    normed = centred * inv_std
    lifted = (normed * norm_gain).astype(jnp.bfloat16).reshape(-1, channels)
    pre = jnp.dot(lifted, w_in, preferred_element_type=jnp.float32)
    cdf = 0.5 * (1.0 + jax.scipy.special.erf(pre * sqrt_half))
    activated = (pre * cdf).astype(jnp.bfloat16)
    mixed = jnp.dot(activated, w_out, preferred_element_type=jnp.float32).reshape(own.shape)
    block_out = own.astype(jnp.float32) + layer_scale * mixed
    weight_live = live * pool_weight
    emb_term = jnp.sum(weight_live[:, None] * jnp.sum(block_out, axis=(1, 2)), axis=0) / tile_side
    extra = pool_weight[:, None] * slide_cot[None, :] / tile_side
    grad_out = live[:, None, None, None] * (upstream.astype(jnp.float32) + extra[:, None, None, :])
    grad_mixed = (grad_out * layer_scale).astype(jnp.bfloat16).reshape(-1, channels)
    grad_act = lax.dot_general(
        grad_mixed, w_out, (((1,), (1,)), ((), ())), preferred_element_type=jnp.float32
    )
    density = jnp.exp(-0.5 * pre * pre) * inv_root_two_pi
    grad_pre = (grad_act * (cdf + pre * density)).astype(jnp.bfloat16)
    grad_lift = lax.dot_general(
        grad_pre, w_in, (((1,), (1,)), ((), ())), preferred_element_type=jnp.float32
    )
    grad_normed = grad_lift.reshape(own.shape) * norm_gain
    grad_conv = inv_std * (
        grad_normed
        - jnp.mean(grad_normed, axis=-1, keepdims=True)
        - normed * jnp.mean(grad_normed * normed, axis=-1, keepdims=True)
    )
    kernel_rows = []
    for row_tap in range(7):
        for col_tap in range(7):
            window = padded[
                :, row_tap : row_tap + tile_side, col_tap : col_tap + tile_side, :
            ].astype(jnp.float32)
            kernel_rows.append(jnp.sum(window * grad_conv, axis=(0, 1, 2)))
    kernel_grad = jnp.stack(kernel_rows).reshape(7, 7, channels)
    return (emb_term, grad_out, grad_conv, activated, grad_mixed, kernel_grad)


def per_device(
    tiles_in,
    upstream,
    pool_weight,
    slide_cot,
    adjacency,
    counts,
    kernel,
    norm_gain,
    w_in,
    w_out,
    layer_scale,
):
    own = tiles_in[0]
    capacity = own.shape[0]
    tile_side = own.shape[1]
    position = lax.axis_index("space")
    own_base = position * capacity
    north_base = own_base - capacity
    south_base = own_base + capacity
    wanted = adjacency[0]
    live = (jnp.arange(capacity, dtype=jnp.int32) < counts[0, 0]).astype(jnp.float32)
    north_rows = passed_along(own[:, tile_side - 3 :], "space", 1)
    south_rows = passed_along(own[:, :3], "space", -1)
    padded = frame(
        own,
        north_rows,
        south_rows,
        own[:, :, tile_side - 3 :],
        own[:, :, :3],
        wanted,
        north_base,
        own_base,
        south_base,
    )
    emb_term, grad_out, grad_conv, activated, grad_mixed, kernel_grad = block_pass(
        padded,
        own,
        upstream[0],
        pool_weight[0],
        live,
        slide_cot[0],
        kernel,
        norm_gain,
        w_in,
        w_out,
        layer_scale,
    )
    embedding = lax.psum(emb_term, "space")
    local_weight = lax.dot_general(
        activated, grad_mixed, (((0,), (0,)), ((), ())), preferred_element_type=jnp.float32
    )
    whole_weight, kernel_dp = (
        lax.psum(local_weight.astype(jnp.bfloat16), "dp").astype(jnp.float32),
        lax.psum(kernel_grad.astype(jnp.bfloat16), "dp").astype(jnp.float32),
    )
    weight_share = lax.psum_scatter(whole_weight, "space", scatter_dimension=0, tiled=True)
    kernel_total = lax.psum(kernel_dp, "space")
    grad_north = passed_along(
        grad_conv[:, tile_side - 3 :].astype(jnp.bfloat16), "space", 1
    ).astype(jnp.float32)
    grad_south = passed_along(grad_conv[:, :3].astype(jnp.bfloat16), "space", -1).astype(
        jnp.float32
    )
    padded_grad = frame(
        grad_conv,
        grad_north,
        grad_south,
        grad_conv[:, :, tile_side - 3 :],
        grad_conv[:, :, :3],
        wanted,
        north_base,
        own_base,
        south_base,
    )
    back = depthwise(padded_grad, kernel[::-1, ::-1], tile_side)
    grad_tiles = ((grad_out + back) * live[:, None, None, None]).astype(jnp.bfloat16)
    return (embedding[None, :], grad_tiles[None], weight_share, kernel_total)


def solution(mesh):
    return jax.shard_map(
        per_device,
        mesh=mesh,
        in_specs=(
            P("dp", "space", None, None, None),
            P("dp", "space", None, None, None),
            P("dp", "space"),
            P("dp", None),
            P("dp", "space", None),
            P("dp", "space"),
            P(),
            P(),
            P(),
            P(),
            P(),
        ),
        out_specs=(P("dp", None), P("dp", "space", None, None, None), P("space", None), P()),
        check_vma=False,
    )
```

profile of v0, /device:TPU:0, one launch (start us, length us, event | category | flops | bytes accessed | tf_op | source)
XLA Modules:
  0.0 189.6 jit_solution(16808455452502542343)
XLA Ops:
  7.2 1.0 fusion.191
  8.3 2.4 %collective-permute-start = (bf16[4,3,8,384]{3,2,1,0:T(8,128)(2,1)S(1)}, bf16[4,3,8,384]{3,2,1,0:T(8,128)(2,1)S(1)}, u32[]{:S(2)}, u32[]{:S(2)}) collective-permute-start(bf16[4,3,8,384]{3,2,1,0:T(8,128)(2,1)S(1)} %get-tuple-element.146), channel_id=1, source_target_pairs={{0,1},{1,2},{2,3},{3,4},{4,5},{5,6},{6,7},{7,8},{8,9},{9,10},{10,1... | collective-permute-start | bytes 221192 | tf_op jit(solution)/shard_map/ppermute | solution.py:13
  10.7 1.3 collective-permute-start.1
  12.0 1.1 fusion.192
  13.1 1.3 compare_reduce_fusion.7
  14.5 1.3 clamp_reduce_fusion.7
  18.1 1.9 %slice_reduce_fusion.48 = (f32[384]{0:T(512)S(1)}, f32[384]{0:T(512)S(1)}, f32[384]{0:T(512)S(1)}, f32[384]{0:T(512)S(1)}, f32[384]{0:T(512)S(1)}, /*index=5*/f3...) fusion(f32[7,7,384]{2,1,0:T(8,128)} %param.25), kind=kLoop, calls=%fused_computation.487 | loop fusion | bytes 58368 | tf_op jit(solution)/shard_map/slice | solution.py:23
  20.1 1.9 slice_reduce_fusion.47
  23.7 1.2 compare_select_fusion.8
  35.5 4.3 %fusion.187 = (f32[4,8,8]{2,1,0:T(8,128)S(1)}, f32[4,8,8,384]{3,2,1,0:T(8,128)S(1)}) fusion(f32[384]{0:T(512)S(1)} %get-tuple-element.114, bf16[4,11,14,384]{3,2,1,0:T(8,128)(2,1)S(1)} %get-tuple-element.143, f32[384]{0:T(512)S(1)} %get-tuple-element.115, f32[384]{0:T(512)S(1)} %get-tuple-element.68, f32[384]{0:T(512)S(1)} %get-tuple-element.69, ...), kind=kLoop, calls=%fused_computation.495 | loop fusion | flops 16219904 | bytes 9071104 | tf_op jit(solution)/shard_map/reduce_sum | solution.py:67
  40.2 2.0 %multiply_convert_fusion = (bf16[256,1536]{1,0:T(8,128)(2,1)}, f32[256,1536]{1,0:T(8,128)}) fusion(bf16[256,384]{1,0:T(8,128)(2,1)S(1)} %bitcast.50, bf16[384,1536]{1,0:T(8,128)(2,1)S(1)} %copy-done), kind=kOutput, calls=%fused_computation.24 | convolution fusion | flops 303955968 | bytes 3735552 | tf_op jit(solution)/shard_map/dot_general | solution.py:71
  42.2 3.1 %multiply_reduce_fusion.1 = (f32[256]{0:T(256)S(1)}, f32[256,384]{1,0:T(8,128)S(1)}) fusion(f32[384]{0:T(512)S(1)} %copy-done.7, bf16[384,1536]{1,0:T(8,128)(2,1)S(1)} %copy-done, bf16[256,384]{1,0:T(8,128)(2,1)} %fusion.169, bf16[1536,384]{1,0:T(8,128)(2,1)} %param.28, f32[256,1536]{1,0:T(8,128)} %get-tuple-element.153), kind=kOutput, calls=%fused_computation.359 | convolution fusion | flops 608108288 | bytes 4524544 | tf_op jit(solution)/shard_map/dot_general | solution.py:86
  45.7 2.8 %convolution_convert_fusion = bf16[1536,384]{1,0:T(8,128)(2,1)} fusion(bf16[256,1536]{1,0:T(8,128)(2,1)} %get-tuple-element.152, bf16[256,384]{1,0:T(8,128)(2,1)} %fusion.169), kind=kOutput, calls=%fused_computation.16 | convolution fusion | flops 302579712 | bytes 2162688 | tf_op jit(solution)/shard_map/dot_general | solution.py:155
  48.6 2.0 %fusion.186 = (bf16[4,8,8,384]{3,2,1,0:T(8,128)(2,1)}, f32[4,8,8,384]{3,2,1,0:T(8,128)S(1)}) fusion(f32[4,8,8]{2,1,0:T(8,128)S(1)} %broadcast_multiply_fusion, f32[4,8,8,384]{3,2,1,0:T(8,128)S(1)} %get-tuple-element.137, f32[4,8,8]{2,1,0:T(8,128)S(1)} %broadcast_multiply_fusion.1, f32[4,8,8]{2,1,0:T(8,128)S(1)} %div.33, f32[384]{0:T(512)S(1)} %copy-done.7, ...), kind=kLoop, calls=%fused_computation.494 | loop fusion | flops 786432 | bytes 1381888 | tf_op jit(solution)/shard_map/convert.101
  50.5 3.1 %fusion.85 = (bf16[384]{0:T(512)(128)(2,1)}, bf16[384]{0:T(512)(128)(2,1)}, bf16[384]{0:T(512)(128)(2,1)}, bf16[384]{0:T(512)(128)(2,1)}, bf16[384]{0:T(512)(128...) fusion(f32[4,8,8,384]{3,2,1,0:T(8,128)S(1)} %get-tuple-element., ...), kind=kOutput, calls=%fused_computation.225 | convolution fusion | flops 306998016 | bytes 3505152 | tf_op jit(solution)/shard_map/dot_general | solution.py:74
  56.1 5.1 %collective-permute-start.2 = (bf16[4,3,8,384]{3,2,1,0:T(8,128)(2,1)}, bf16[4,3,8,384]{3,2,1,0:T(8,128)(2,1)S(1)}, u32[]{:S(2)}, u32[]{:S(2)}) collective-permute-start(bf16[4,3,8,384]{3,2,1,0:T(8,128)(2,1)} %get-tuple-element.144), channel_id=1, source_target_pairs={{0,1},{1,2},{2,3},{3,4},{4,5},{5,6},{6,7},{7,8},{8,9},{9,10},{10,1... | collective-permute-start | bytes 221192 | tf_op jit(solution)/shard_map/ppermute | solution.py:13
  61.2 1.5 collective-permute-start.3
  65.0 31.3 %all-reduce.4.cloned.1.call-done = bf16[1536,384]{1,0:T(8,128)(2,1)} async-done(((bf16[1536,384]{1,0:T(8,128)(2,1)}), bf16[1536,384]{1,0:T(8,128)(2,1)}) %all-reduce.4.cloned.1.call-update) | async-done | bytes 1179664 | tf_op jit(solution)/shard_map/psum | solution.py:159
  96.2 2.8 %convert_element_type.315 = f32[1536,384]{1,0:T(8,128)} convert(bf16[1536,384]{1,0:T(8,128)(2,1)} %all-reduce.4.cloned.1.call-done) | non-fusion elementwise | flops 589824 | bytes 3538944 | tf_op jit(solution)/shard_map/convert_element_type | solution.py:159
  99.1 1.0 fusion.53
  100.2 1.0 fusion.103
  102.3 7.4 %psum.30 = bf16[7,7,384]{2,1,0:T(8,128)(2,1)S(1)} all-reduce(bf16[7,7,384]{2,1,0:T(8,128)(2,1)S(1)} %convert_element_type.316), channel_id=1, replica_groups=mesh['dp'=2,'space'=16] {'dp'}, use_global_device_ids=true, to_apply=%region_58.63 | all-reduce | flops 18816 | bytes 75264 | tf_op jit(solution)/shard_map/psum | solution.py:160
  109.8 61.0 %all-reduce.5 = (f32[1,384]{1,0:T(1,128)}, f32[7,7,384]{2,1,0:T(8,128)}) all-reduce(f32[1,384]{1,0:T(1,128)S(1)} %broadcast_in_dim.154, bf16[7,7,384]{2,1,0:T(8,128)(2,1)S(1)} %psum.30), channel_id=1, replica_groups=mesh['dp'=2,'space'=16] {'space'}, use_global_device_ids=true, to_apply=%region_4.7 | all-reduce | flops 19200 | bytes 115968 | tf_op jit(solution)/shard_map/psum | solution.py:154
  178.3 4.4 %fusion.175 = bf16[1,4,8,8,384]{4,3,2,1,0:T(8,128)(2,1)} fusion(f32[384]{0:T(512)S(1)} %copy-done.19, f32[4,11,14,384]{3,2,1,0:T(8,128)S(1)} %get-tuple-element.139, f32[384]{0:T(512)S(1)} %copy-done.54, f32[384]{0:T(512)S(1)} %get-tuple-element.105, f32[384]{0:T(512)S(1)} %copy-done.13, f32[384]{0:T(512)S(1)} %copy-done.11, f32[384]{0:T(512)S(1)} %copy-done.9, ...), kind=kLoop, calls=%fused_computation.371 | loop fusion | flops 10715136 | bytes 17677840 | tf_op jit(solution)/shard_map/broadcast_in_dim | solution.py:183
  (358 shorter events, 26.3 us)
Async XLA Ops:
  7.2 33.0 %copy-start = (bf16[384,1536]{1,0:T(8,128)(2,1)S(1)}, bf16[384,1536]{1,0:T(8,128)(2,1)}, u32[]{:S(2)}) copy-start(bf16[384,1536]{1,0:T(8,128)(2,1)} %param.27) | copy-start | bytes 3538948
  7.2 21.3 %copy-start.69 = (f32[384]{0:T(512)S(1)}, f32[384]{0:T(512)}, u32[]{:S(2)}) copy-start(f32[384]{0:T(512)} %param.29) | copy-start | bytes 4612
  7.2 21.3 %copy-start.4 = (bf16[1,4,8,8,384]{4,3,2,1,0:T(8,128)(2,1)S(1)}, bf16[1,4,8,8,384]{4,3,2,1,0:T(8,128)(2,1)}, u32[]{:S(2)}) copy-start(bf16[1,4,8,8,384]{4,3,2,1,0:T(8,128)(2,1)} %param.20) | copy-start | bytes 589828
  7.2 89.0 %all-reduce.4.cloned.1.call-start = ((), (), s32[]{:S(2)}) async-start(), calls=%async_computation.1 | async-start | bytes 2359296 | tf_op jit(solution)/shard_map/psum | solution.py:159
  8.3 21.0 %collective-permute-start = (bf16[4,3,8,384]{3,2,1,0:T(8,128)(2,1)S(1)}, bf16[4,3,8,384]{3,2,1,0:T(8,128)(2,1)S(1)}, u32[]{:S(2)}, u32[]{:S(2)}) collective-permute-start(bf16[4,3,8,384]{3,2,1,0:T(8,128)(2,1)S(1)} %get-tuple-element.146), channel_id=1, source_target_pairs={{0,1},{1,2},{2,3},{3,4},{4,5},{5,6},{6,7},{7,8},{8,9},{9,10},{10,1... | collective-permute-start | bytes 221192 | tf_op jit(solution)/shard_map/ppermute | solution.py:13
  10.7 21.3 %collective-permute-start.1 = (bf16[4,3,8,384]{3,2,1,0:T(8,128)(2,1)S(1)}, bf16[4,3,8,384]{3,2,1,0:T(8,128)(2,1)S(1)}, u32[]{:S(2)}, u32[]{:S(2)}) collective-permute-start(bf16[4,3,8,384]{3,2,1,0:T(8,128)(2,1)S(1)} %get-tuple-element.147), channel_id=1, source_target_pairs={{1,0},{2,1},{3,2},{4,3},{5,4},{6,5},{7,6},{8,7},{9,8},{10,9},{11,1... | collective-permute-start | bytes 221192 | tf_op jit(solution)/shard_map/ppermute | solution.py:13
  14.4 18.2 %copy-start.81 = (pred[4]{0:T(512)(128)(4,1)}, pred[4]{0:T(512)(128)(4,1)S(1)}, u32[]{:S(2)}) copy-start(pred[4]{0:T(512)(128)(4,1)S(1)} %get-tuple-element.123) | copy-start | bytes 16
  14.4 18.2 %copy-start.87 = (pred[4]{0:T(512)(128)(4,1)}, pred[4]{0:T(512)(128)(4,1)S(1)}, u32[]{:S(2)}) copy-start(pred[4]{0:T(512)(128)(4,1)S(1)} %get-tuple-element.116) | copy-start | bytes 16
  14.4 18.2 %copy-start.89 = (pred[4]{0:T(512)(128)(4,1)}, pred[4]{0:T(512)(128)(4,1)S(1)}, u32[]{:S(2)}) copy-start(pred[4]{0:T(512)(128)(4,1)S(1)} %get-tuple-element.122) | copy-start | bytes 16
  14.4 18.2 %copy-start.91 = (pred[4]{0:T(512)(128)(4,1)}, pred[4]{0:T(512)(128)(4,1)S(1)}, u32[]{:S(2)}) copy-start(pred[4]{0:T(512)(128)(4,1)S(1)} %get-tuple-element.121) | copy-start | bytes 16
  14.5 18.2 %copy-start.92 = (pred[4]{0:T(512)(128)(4,1)}, pred[4]{0:T(512)(128)(4,1)S(1)}, u32[]{:S(2)}) copy-start(pred[4]{0:T(512)(128)(4,1)S(1)} %get-tuple-element.120) | copy-start | bytes 16
  14.5 18.2 %copy-start.85 = (pred[4]{0:T(512)(128)(4,1)}, pred[4]{0:T(512)(128)(4,1)S(1)}, u32[]{:S(2)}) copy-start(pred[4]{0:T(512)(128)(4,1)S(1)} %get-tuple-element.117) | copy-start | bytes 16
  14.5 18.9 %copy-start.79 = (pred[4]{0:T(512)(128)(4,1)}, pred[4]{0:T(512)(128)(4,1)S(1)}, u32[]{:S(2)}) copy-start(pred[4]{0:T(512)(128)(4,1)S(1)} %get-tuple-element.118) | copy-start | bytes 16
  14.5 19.6 %copy-start.83 = (pred[4]{0:T(512)(128)(4,1)}, pred[4]{0:T(512)(128)(4,1)S(1)}, u32[]{:S(2)}) copy-start(pred[4]{0:T(512)(128)(4,1)S(1)} %get-tuple-element.119) | copy-start | bytes 16
  15.8 17.6 %copy-start.93 = (pred[4]{0:T(512)(128)(4,1)}, pred[4]{0:T(512)(128)(4,1)S(1)}, u32[]{:S(2)}) copy-start(pred[4]{0:T(512)(128)(4,1)S(1)} %get-tuple-element.161) | copy-start | bytes 16
  18.0 17.3 %copy-start.8 = (f32[384]{0:T(512)}, f32[384]{0:T(512)S(1)}, u32[]{:S(2)}) copy-start(f32[384]{0:T(512)S(1)} %get-tuple-element.111) | copy-start | bytes 4612
  18.0 17.3 %copy-start.10 = (f32[384]{0:T(512)}, f32[384]{0:T(512)S(1)}, u32[]{:S(2)}) copy-start(f32[384]{0:T(512)S(1)} %get-tuple-element.112) | copy-start | bytes 4612
  18.1 17.3 %copy-start.12 = (f32[384]{0:T(512)}, f32[384]{0:T(512)S(1)}, u32[]{:S(2)}) copy-start(f32[384]{0:T(512)S(1)} %get-tuple-element.113) | copy-start | bytes 4612
  18.1 17.3 %copy-start.14 = (f32[384]{0:T(512)}, f32[384]{0:T(512)S(1)}, u32[]{:S(2)}) copy-start(f32[384]{0:T(512)S(1)} %get-tuple-element.114) | copy-start | bytes 4612
  18.1 17.3 %copy-start.16 = (f32[384]{0:T(512)}, f32[384]{0:T(512)S(1)}, u32[]{:S(2)}) copy-start(f32[384]{0:T(512)S(1)} %get-tuple-element.115) | copy-start | bytes 4612
  48.5 134.3 %reduce-scatter.2.cloned.1.call-start = ((), (), s32[]{:S(2)}) async-start(), calls=%async_computation.2 | async-start | bytes 2506752 | tf_op jit(solution)/shard_map/reduce_scatter | solution.py:162
  56.1 114.7 %collective-permute-start.2 = (bf16[4,3,8,384]{3,2,1,0:T(8,128)(2,1)}, bf16[4,3,8,384]{3,2,1,0:T(8,128)(2,1)S(1)}, u32[]{:S(2)}, u32[]{:S(2)}) collective-permute-start(bf16[4,3,8,384]{3,2,1,0:T(8,128)(2,1)} %get-tuple-element.144), channel_id=1, source_target_pairs={{0,1},{1,2},{2,3},{3,4},{4,5},{5,6},{6,7},{7,8},{8,9},{9,10},{10,1... | collective-permute-start | bytes 221192 | tf_op jit(solution)/shard_map/ppermute | solution.py:13
  61.2 111.7 %collective-permute-start.3 = (bf16[4,3,8,384]{3,2,1,0:T(8,128)(2,1)S(1)}, bf16[4,3,8,384]{3,2,1,0:T(8,128)(2,1)S(1)}, u32[]{:S(2)}, u32[]{:S(2)}) collective-permute-start(bf16[4,3,8,384]{3,2,1,0:T(8,128)(2,1)S(1)} %get-tuple-element.145), channel_id=1, source_target_pairs={{1,0},{2,1},{3,2},{4,3},{5,4},{6,5},{7,6},{8,7},{9,8},{10,9},{11,1... | collective-permute-start | bytes 221192 | tf_op jit(solution)/shard_map/ppermute | solution.py:13
  102.3 72.7 %copy-start.90 = (pred[4]{0:T(512)(128)(4,1)S(1)}, pred[4]{0:T(512)(128)(4,1)}, u32[]{:S(2)}) copy-start(pred[4]{0:T(512)(128)(4,1)} %copy-done.89) | copy-start | bytes 16
  (94 other events, 460.1 us)
Sparse Core Ops, SparseCore 0:
  48.6 47.5 all-reduce.3
  100.6 63.7 reduce-scatter.1
where the time goes:
time: 191 us; the launch traced here: 190 us
  blocking collectives  68.5 us (36%)
  other arithmetic  31.7 us (17%)
  waiting for transfers between devices  31.3 us (16%)
  local copies, waits for them, and re-layouts  19.6 us (10%)
  between operations  17.1 us (9%)
  matrix products  11 us (6%)
  starting transfers between devices  10.4 us (5%)
    psum x1, blocking collectives, per_device(): embedding = lax.psum(emb_term, 'space')  61 us
    psum x1, waiting for transfers between devices, per_device(): lax.psum(local_weight.astype(jnp.bfloat16), 'dp').astype(jnp.float32)  31.3 us
    gather x16, local copies, waits for them, and re-layouts, pick(): chosen = jnp.take(source, index, axis=0)  10.5 us
    ppermute x4, starting transfers between devices, passed_along(): lax.ppermute(value, axis, [(source, source + steps) for source in range(l...  10.3 us
    psum x1, blocking collectives, per_device(): lax.psum(kernel_grad.astype(jnp.bfloat16), 'dp').astype(jnp.float32)  7.44 us
    select_n x16, other arithmetic, pick(): return jnp.where(valid[:, None, None, None], chosen, jnp.zeros_like(chosen))  6.9 us
    slice x3, local copies, waits for them, and re-layouts, depthwise(): total = total + window * kernel[row_tap, col_tap]  4.74 us
    broadcast_in_dim x1, other arithmetic, per_device(): return (embedding[None, :], grad_tiles[None], weight_share, kernel_total)  4.44 us
  transfers between devices with their start and end apart: 6, of which 1 were waited for; matrix products, arithmetic and copies ran while one was open for 24% of the time, Pallas kernels for 0%

commit v1 on v0

--- a/solution.py
+++ b/solution.py
@@ -151,7 +151,7 @@
         w_out,
         layer_scale,
     )
-    embedding = lax.psum(emb_term, "space")
+    embedding = jnp.sum(lax.all_gather(emb_term, "space"), axis=0)
     local_weight = lax.dot_general(
         activated, grad_mixed, (((0,), (0,)), ((), ())), preferred_element_type=jnp.float32
     )

time: 191 us -> 239 us (1.25)
  blocking collectives: 68.5 us -> 88.6 us
  other arithmetic: 31.7 us -> 41.9 us
  local copies, waits for them, and re-layouts: 19.6 us -> 29 us
  waiting for transfers between devices: 31.3 us -> 40.1 us
    all_gather x0 -> x1, blocking collectives: none -> 21.9 us  [per_device(): embedding = jnp.sum(lax.all_gather(emb_term, 'space'), axis=0)]
    psum x1, waiting for transfers between devices: 31.3 us -> 40.1 us  [per_device(): lax.psum(local_weight.astype(jnp.bfloat16), 'dp').astype(jnp.float32)]
    select_n x16, other arithmetic: 6.9 us -> 12 us  [pick(): return jnp.where(valid[:, None, None, None], chosen, jnp.zeros_like(chosen))]
    gather x8, other arithmetic: 0.05 us -> 3.58 us
    another operation x50, local copies, waits for them, and re-layouts: 0.48 us -> 3.74 us  [block_pass(): kernel_grad = jnp.stack(kernel_rows).reshape(7, 7, channels)]
    reduce_sum x3, other arithmetic: 2.17 us -> 4.95 us  [block_pass(): kernel_rows.append(jnp.sum(window * grad_conv, axis=(0, 1, 2)))]
    gather x16, local copies, waits for them, and re-layouts: 10.5 us -> 13 us  [pick(): chosen = jnp.take(source, index, axis=0)]
where the time goes in v1:
time: 239 us; the launch traced here: 238 us
  blocking collectives  88.6 us (37%)
  other arithmetic  41.9 us (18%)
  waiting for transfers between devices  40.1 us (17%)
  local copies, waits for them, and re-layouts  29 us (12%)
  between operations  17.3 us (7%)
  matrix products  11.8 us (5%)
  starting transfers between devices  8.9 us (4%)
    psum x1, blocking collectives, per_device(): kernel_total = lax.psum(kernel_dp, 'space')  59.3 us
    psum x1, waiting for transfers between devices, per_device(): lax.psum(local_weight.astype(jnp.bfloat16), 'dp').astype(jnp.float32)  40.1 us
    all_gather x1, blocking collectives, per_device(): embedding = jnp.sum(lax.all_gather(emb_term, 'space'), axis=0)  21.9 us
    gather x16, local copies, waits for them, and re-layouts, pick(): chosen = jnp.take(source, index, axis=0)  13 us
    select_n x16, other arithmetic, pick(): return jnp.where(valid[:, None, None, None], chosen, jnp.zeros_like(chosen))  12 us
    ppermute x4, starting transfers between devices, passed_along(): lax.ppermute(value, axis, [(source, source + steps) for source in range(l...  8.82 us
    psum x1, blocking collectives, per_device(): lax.psum(kernel_grad.astype(jnp.bfloat16), 'dp').astype(jnp.float32)  7.44 us
    reduce_sum x3, other arithmetic, block_pass(): kernel_rows.append(jnp.sum(window * grad_conv, axis=(0, 1, 2)))  4.95 us
  transfers between devices with their start and end apart: 6, of which 1 were waited for; matrix products, arithmetic and copies ran while one was open for 24% of the time, Pallas kernels for 0%

profile of v1, /device:TPU:0, one launch (start us, length us, event | category | flops | bytes accessed | tf_op | source)
XLA Modules:
  0.0 237.6 jit_solution(13310036319751499531)
XLA Ops:
  8.3 1.3 collective-permute-start.1
  9.6 3.0 %collective-permute-start = (bf16[4,3,8,384]{3,2,1,0:T(8,128)(2,1)S(1)}, bf16[4,3,8,384]{3,2,1,0:T(8,128)(2,1)S(1)}, u32[]{:S(2)}, u32[]{:S(2)}) collective-permute-start(bf16[4,3,8,384]{3,2,1,0:T(8,128)(2,1)S(1)} %get-tuple-element.144), channel_id=1, source_target_pairs={{0,1},{1,2},{2,3},{3,4},{4,5},{5,6},{6,7},{7,8},{8,9},{9,10},{10,1... | collective-permute-start | bytes 221192 | tf_op jit(solution)/shard_map/ppermute | solution.py:13
  13.8 1.9 compare_reduce_fusion.7
  15.6 1.3 clamp_reduce_fusion.7
  20.7 1.8 slice_reduce_fusion.48
  22.6 1.6 slice_reduce_fusion.46
  43.8 4.1 %fusion.186 = (f32[4,8,8]{2,1,0:T(8,128)S(1)}, f32[4,8,8,384]{3,2,1,0:T(8,128)S(1)}) fusion(f32[384]{0:T(512)} %get-tuple-element.114, bf16[4,11,14,384]{3,2,1,0:T(8,128)(2,1)S(1)} %get-tuple-element.141, f32[384]{0:T(512)} %get-tuple-element.115, f32[384]{0:T(512)S(1)} %get-tuple-element.68, f32[384]{0:T(512)S(1)} %get-tuple-element.69, ...), kind=kLoop, calls=%fused_computation.494 | loop fusion | flops 16219904 | bytes 9071104 | tf_op jit(solution)/shard_map/reduce_sum | solution.py:67
  48.3 2.0 multiply_convert_fusion
  50.3 3.1 %multiply_reduce_fusion.1 = (f32[256]{0:T(256)S(1)}, f32[256,384]{1,0:T(8,128)S(1)}) fusion(f32[384]{0:T(512)S(1)} %copy-done.10, bf16[384,1536]{1,0:T(8,128)(2,1)S(1)} %copy-done, bf16[256,384]{1,0:T(8,128)(2,1)S(1)} %copy-done.6, bf16[1536,384]{1,0:T(8,128)(2,1)} %param.28, f32[256,1536]{1,0:T(8,128)} %get-tuple-element.151), kind=kOutput, calls=%fused_computation.359 | convolution fusion | flops 608108288 | bytes 4524544 | tf_op jit(solution)/shard_map/dot_general | solution.py:86
  54.2 2.7 %convolution_convert_fusion = bf16[1536,384]{1,0:T(8,128)(2,1)} fusion(bf16[256,1536]{1,0:T(8,128)(2,1)} %get-tuple-element.150, bf16[256,384]{1,0:T(8,128)(2,1)S(1)} %copy-done.6), kind=kOutput, calls=%fused_computation.16 | convolution fusion | flops 302579712 | bytes 2162688 | tf_op jit(solution)/shard_map/dot_general | solution.py:155
  57.7 2.5 %fusion.103 = (bf16[384]{0:T(512)(128)(2,1)}, bf16[384]{0:T(512)(128)(2,1)}, bf16[384]{0:T(512)(128)(2,1)}, bf16[384]{0:T(512)(128)(2,1)}, bf16[384]{0:T(512)(12...) fusion(bf16[4,11,14,384]{3,2,1,0:T(8,128)(2,1)S(1)} %get-tuple-, ...), kind=kLoop, calls=%fused_computation.243 | loop fusion | flops 5989632 | bytes 4738048 | tf_op jit(solution)/shard_map/reduce_sum | solution.py:101
  61.1 2.2 fusion.53
  63.3 40.1 %all-reduce.3.cloned.1.call-done = bf16[1536,384]{1,0:T(8,128)(2,1)} async-done(((bf16[1536,384]{1,0:T(8,128)(2,1)}), bf16[1536,384]{1,0:T(8,128)(2,1)}) %all-reduce.3.cloned.1.call-update) | async-done | bytes 1179664 | tf_op jit(solution)/shard_map/psum | solution.py:159
  103.4 2.8 %convert_element_type.315 = f32[1536,384]{1,0:T(8,128)} convert(bf16[1536,384]{1,0:T(8,128)(2,1)} %all-reduce.3.cloned.1.call-done) | non-fusion elementwise | flops 589824 | bytes 3538944 | tf_op jit(solution)/shard_map/convert_element_type | solution.py:159
  106.3 1.7 fusion.189
  108.0 4.0 %fusion.85 = (bf16[384]{0:T(512)(128)(2,1)}, bf16[384]{0:T(512)(128)(2,1)}, bf16[384]{0:T(512)(128)(2,1)}, bf16[384]{0:T(512)(128)(2,1)}, bf16[384]{0:T(512)(128...) fusion(f32[4,8,8,384]{3,2,1,0:T(8,128)S(1)} %get-tuple-element., ...), kind=kOutput, calls=%fused_computation.225 | convolution fusion | flops 306998016 | bytes 3505152 | tf_op jit(solution)/shard_map/dot_general | solution.py:74
  112.0 1.3 collective-permute-start.3
  113.2 3.2 %collective-permute-start.2 = (bf16[4,3,8,384]{3,2,1,0:T(8,128)(2,1)}, bf16[4,3,8,384]{3,2,1,0:T(8,128)(2,1)S(1)}, u32[]{:S(2)}, u32[]{:S(2)}) collective-permute-start(bf16[4,3,8,384]{3,2,1,0:T(8,128)(2,1)} %get-tuple-element.142), channel_id=1, source_target_pairs={{0,1},{1,2},{2,3},{3,4},{4,5},{5,6},{6,7},{7,8},{8,9},{9,10},{10,1... | collective-permute-start | bytes 221192 | tf_op jit(solution)/shard_map/ppermute | solution.py:13
  116.5 1.7 gather_fusion.11
  118.6 1.7 gather_fusion.12
  127.2 7.4 %psum.22 = bf16[7,7,384]{2,1,0:T(8,128)(2,1)S(1)} all-reduce(bf16[7,7,384]{2,1,0:T(8,128)(2,1)S(1)} %convert_element_type.316), channel_id=1, replica_groups=mesh['dp'=2,'space'=16] {'dp'}, use_global_device_ids=true, to_apply=%region_58.63 | all-reduce | flops 18816 | bytes 75264 | tf_op jit(solution)/shard_map/psum | solution.py:160
  134.7 21.9 %all-gather.1 = f32[16,1,384]{2,1,0:T(1,128)S(1)} all-gather(f32[1,1,384]{2,1,0:T(1,128)S(1)} %reshape.470), channel_id=2, replica_groups=mesh['dp'=2,'space'=16] {'space'}, dimensions={0}, use_global_device_ids=true | all-gather | bytes 26112 | tf_op jit(solution)/shard_map/all_gather | solution.py:154
  157.2 59.3 %all-reduce.4 = f32[7,7,384]{2,1,0:T(8,128)} all-reduce(bf16[7,7,384]{2,1,0:T(8,128)(2,1)S(1)} %psum.22), channel_id=1, replica_groups=mesh['dp'=2,'space'=16] {'space'}, use_global_device_ids=true, to_apply=%region_59.64 | all-reduce | flops 18816 | bytes 112896 | tf_op jit(solution)/shard_map/psum | solution.py:163
  226.4 4.4 %fusion.175 = bf16[1,4,8,8,384]{4,3,2,1,0:T(8,128)(2,1)} fusion(f32[384]{0:T(512)S(1)} %copy-done.50, f32[4,11,14,384]{3,2,1,0:T(8,128)S(1)} %get-tuple-element.136, f32[384]{0:T(512)S(1)} %copy-done.12, f32[384]{0:T(512)} %get-tuple-element.105, f32[384]{0:T(512)} %get-tuple-element.113, f32[384]{0:T(512)} %get-tuple-element.112, ...), kind=kLoop, calls=%fused_computation.371 | loop fusion | flops 10715136 | bytes 17677840 | tf_op jit(solution)/shard_map/broadcast_in_dim | solution.py:183
  (398 shorter events, 43.2 us)
Async XLA Ops:
  7.2 41.1 %copy-start = (bf16[384,1536]{1,0:T(8,128)(2,1)S(1)}, bf16[384,1536]{1,0:T(8,128)(2,1)}, u32[]{:S(2)}) copy-start(bf16[384,1536]{1,0:T(8,128)(2,1)} %param.27) | copy-start | bytes 3538948
  7.2 23.5 %copy-start.129 = (f32[1,384]{1,0:T(1,128)S(1)}, f32[1,384]{1,0:T(1,128)}, u32[]{:S(2)}) copy-start(f32[1,384]{1,0:T(1,128)} %param.22) | copy-start | bytes 4612
  7.2 23.5 %copy-start.130 = (f32[1,4]{1,0:T(1,128)S(1)}, f32[1,4]{1,0:T(1,128)}, u32[]{:S(2)}) copy-start(f32[1,4]{1,0:T(1,128)} %param.21) | copy-start | bytes 52
  7.2 25.7 %copy-start.4 = (bf16[1,4,8,8,384]{4,3,2,1,0:T(8,128)(2,1)S(1)}, bf16[1,4,8,8,384]{4,3,2,1,0:T(8,128)(2,1)}, u32[]{:S(2)}) copy-start(bf16[1,4,8,8,384]{4,3,2,1,0:T(8,128)(2,1)} %param.20) | copy-start | bytes 589828
  7.2 25.7 %copy-start.85 = (f32[384]{0:T(512)S(1)}, f32[384]{0:T(512)}, u32[]{:S(2)}) copy-start(f32[384]{0:T(512)} %param.29) | copy-start | bytes 4612
  7.2 96.2 %all-reduce.3.cloned.1.call-start = ((), (), s32[]{:S(2)}) async-start(), calls=%async_computation.1 | async-start | bytes 2359296 | tf_op jit(solution)/shard_map/psum | solution.py:159
  8.3 25.9 %collective-permute-start.1 = (bf16[4,3,8,384]{3,2,1,0:T(8,128)(2,1)S(1)}, bf16[4,3,8,384]{3,2,1,0:T(8,128)(2,1)S(1)}, u32[]{:S(2)}, u32[]{:S(2)}) collective-permute-start(bf16[4,3,8,384]{3,2,1,0:T(8,128)(2,1)S(1)} %get-tuple-element.145), channel_id=1, source_target_pairs={{1,0},{2,1},{3,2},{4,3},{5,4},{6,5},{7,6},{8,7},{9,8},{10,9},{11,1... | collective-permute-start | bytes 221192 | tf_op jit(solution)/shard_map/ppermute | solution.py:13
  9.6 26.1 %collective-permute-start = (bf16[4,3,8,384]{3,2,1,0:T(8,128)(2,1)S(1)}, bf16[4,3,8,384]{3,2,1,0:T(8,128)(2,1)S(1)}, u32[]{:S(2)}, u32[]{:S(2)}) collective-permute-start(bf16[4,3,8,384]{3,2,1,0:T(8,128)(2,1)S(1)} %get-tuple-element.144), channel_id=1, source_target_pairs={{0,1},{1,2},{2,3},{3,4},{4,5},{5,6},{6,7},{7,8},{8,9},{9,10},{10,1... | collective-permute-start | bytes 221192 | tf_op jit(solution)/shard_map/ppermute | solution.py:13
  20.5 22.9 %copy-start.11 = (f32[384]{0:T(512)}, f32[384]{0:T(512)S(1)}, u32[]{:S(2)}) copy-start(f32[384]{0:T(512)S(1)} %get-tuple-element.86) | copy-start | bytes 4612
  20.5 22.9 %copy-start.13 = (f32[384]{0:T(512)}, f32[384]{0:T(512)S(1)}, u32[]{:S(2)}) copy-start(f32[384]{0:T(512)S(1)} %get-tuple-element.87) | copy-start | bytes 4612
  20.5 22.9 %copy-start.15 = (f32[384]{0:T(512)}, f32[384]{0:T(512)S(1)}, u32[]{:S(2)}) copy-start(f32[384]{0:T(512)S(1)} %get-tuple-element.88) | copy-start | bytes 4612
  20.5 22.9 %copy-start.17 = (f32[384]{0:T(512)}, f32[384]{0:T(512)S(1)}, u32[]{:S(2)}) copy-start(f32[384]{0:T(512)S(1)} %get-tuple-element.89) | copy-start | bytes 4612
  20.6 22.9 %copy-start.19 = (f32[384]{0:T(512)}, f32[384]{0:T(512)S(1)}, u32[]{:S(2)}) copy-start(f32[384]{0:T(512)S(1)} %get-tuple-element.90) | copy-start | bytes 4612
  20.6 22.9 %copy-start.21 = (f32[384]{0:T(512)}, f32[384]{0:T(512)S(1)}, u32[]{:S(2)}) copy-start(f32[384]{0:T(512)S(1)} %get-tuple-element.91) | copy-start | bytes 4612
  20.6 22.9 %copy-start.23 = (f32[384]{0:T(512)}, f32[384]{0:T(512)S(1)}, u32[]{:S(2)}) copy-start(f32[384]{0:T(512)S(1)} %get-tuple-element.92) | copy-start | bytes 4612
  20.6 22.9 %copy-start.25 = (f32[384]{0:T(512)}, f32[384]{0:T(512)S(1)}, u32[]{:S(2)}) copy-start(f32[384]{0:T(512)S(1)} %get-tuple-element.93) | copy-start | bytes 4612
  20.6 22.9 %copy-start.27 = (f32[384]{0:T(512)}, f32[384]{0:T(512)S(1)}, u32[]{:S(2)}) copy-start(f32[384]{0:T(512)S(1)} %get-tuple-element.94) | copy-start | bytes 4612
  20.6 22.9 %copy-start.29 = (f32[384]{0:T(512)}, f32[384]{0:T(512)S(1)}, u32[]{:S(2)}) copy-start(f32[384]{0:T(512)S(1)} %get-tuple-element.95) | copy-start | bytes 4612
  20.6 22.9 %copy-start.31 = (f32[384]{0:T(512)}, f32[384]{0:T(512)S(1)}, u32[]{:S(2)}) copy-start(f32[384]{0:T(512)S(1)} %get-tuple-element.96) | copy-start | bytes 4612
  20.6 22.9 %copy-start.33 = (f32[384]{0:T(512)}, f32[384]{0:T(512)S(1)}, u32[]{:S(2)}) copy-start(f32[384]{0:T(512)S(1)} %get-tuple-element.97) | copy-start | bytes 4612
  20.6 22.9 %copy-start.35 = (f32[384]{0:T(512)}, f32[384]{0:T(512)S(1)}, u32[]{:S(2)}) copy-start(f32[384]{0:T(512)S(1)} %get-tuple-element.98) | copy-start | bytes 4612
  57.0 173.8 %reduce-scatter.2.cloned.1.call-start = ((), (), s32[]{:S(2)}) async-start(), calls=%async_computation.2 | async-start | bytes 2506752 | tf_op jit(solution)/shard_map/reduce_scatter | solution.py:162
  112.0 104.5 %collective-permute-start.3 = (bf16[4,3,8,384]{3,2,1,0:T(8,128)(2,1)}, bf16[4,3,8,384]{3,2,1,0:T(8,128)(2,1)S(1)}, u32[]{:S(2)}, u32[]{:S(2)}) collective-permute-start(bf16[4,3,8,384]{3,2,1,0:T(8,128)(2,1)} %get-tuple-element.143), channel_id=1, source_target_pairs={{1,0},{2,1},{3,2},{4,3},{5,4},{6,5},{7,6},{8,7},{9,8},{10,9},{11,1... | collective-permute-start | bytes 221192 | tf_op jit(solution)/shard_map/ppermute | solution.py:13
  113.2 105.3 %collective-permute-start.2 = (bf16[4,3,8,384]{3,2,1,0:T(8,128)(2,1)}, bf16[4,3,8,384]{3,2,1,0:T(8,128)(2,1)S(1)}, u32[]{:S(2)}, u32[]{:S(2)}) collective-permute-start(bf16[4,3,8,384]{3,2,1,0:T(8,128)(2,1)} %get-tuple-element.142), channel_id=1, source_target_pairs={{0,1},{1,2},{2,3},{3,4},{4,5},{5,6},{6,7},{7,8},{8,9},{9,10},{10,1... | collective-permute-start | bytes 221192 | tf_op jit(solution)/shard_map/ppermute | solution.py:13
  (113 other events, 852.6 us)
Sparse Core Ops, SparseCore 0:
  57.1 46.2 all-reduce.2
  107.8 63.3 reduce-scatter.1
